TPU v7x, 128 devices: a whole 4x4x4 slice. The times are simulated.
128 devices in a mesh: dp: 4 (over z), latent: 32 (over x, y, core).
Axes of the slice: x: 4, y: 4, z: 4, core: 2. Of those that a mesh axis runs over, the one named last changes fastest.
Arguments:
- acts: bfloat16 [640, 8192], P(('dp', 'latent')), may hold values from -6 to 6
- chat_len: int32 [128], P(('dp', 'latent')), may hold values from 1 to 5, as said below
- group_of: int32 [640, 1], P(('dp', 'latent')), may hold values from 0 to 4; in each aligned block of 5 rows (0 to 4, 5 to 9, ...) no two rows name the same one
- w_enc: bfloat16 [2, 4096, 16384], P(None, None, 'latent'), may hold values from -0.0625 to 0.0625
- b_enc: float32 [16384], P('latent'), may hold values from -3 to 3
- w_dec: bfloat16 [16384, 8192], P('latent'), may hold values from -0.046875 to 0.046875
- b_dec: float32 [2, 4096], replicated, may hold values from -3 to 3
Outputs:
- grad_enc: bfloat16 [2, 4096, 16384], P(None, 'dp', 'latent')
- grad_dec: bfloat16 [16384, 8192], P('latent', 'dp')
- loss: float32 [], replicated
Inputs may be any that keep to these rules, and one draw needn't show every extreme that they name: `chat_len`: the last serving shard harvests all 5 rows. `group_of`: among the 5 row slots of each serving shard every value 0 to 4 appears exactly once.
All inputs are finite; a program needn't handle non-finite values.
Results may differ from a plain program's by a relative error of at most 0.02.
Values may be sent and summed in bfloat16 or wider, within the bound.
No kernel may reach another device: no remote copies, remote signals or barrier semaphores. Data moves between devices by JAX's collectives and lax.ppermute only.
A program may use at most 128 MiB of HBM per device.

v0:
```python
import jax
import jax.numpy as jnp
from jax import lax
from jax.sharding import PartitionSpec as P

sparsity_weight = 1.0
loss_scale = 8.0
norm_eps = 1e-06


def shards(acts, chat_len, group_of, w_enc, b_enc, w_dec, b_dec):
    groups = lax.axis_size("dp")
    slots = acts.shape[0]
    width = acts.shape[1]
    half = width // 2
    local_latents = w_enc.shape[2]
    capacity = slots // (groups + 1)
    slot_ids = jnp.arange(slots, dtype=jnp.int32)
    alive = (slot_ids < chat_len[0]).astype(jnp.float32)
    order = jnp.argsort(group_of[:, 0], stable=True)[: groups * capacity]
    own_count = jnp.sum(alive[order])
    outgoing = acts[order].reshape(groups, capacity, width)
    out_mask = alive[order].reshape(groups, capacity).astype(jnp.bfloat16)
    received, recv_mask = (
        lax.all_to_all(outgoing, "dp", split_axis=0, concat_axis=0, tiled=True),
        lax.all_to_all(out_mask, "dp", split_axis=0, concat_axis=0, tiled=True),
    )
    member_rows, member_mask = (
        lax.all_gather(received, "latent", axis=0, tiled=True),
        lax.all_gather(recv_mask, "latent", axis=0, tiled=True),
    )
    xg = member_rows.reshape(-1, width)
    maskg = member_mask.reshape(-1).astype(jnp.float32)
    total_rows = xg.shape[0]
    share_rows = total_rows // lax.axis_size("latent")
    first_row = lax.axis_index("latent") * share_rows
    wenc_flat = w_enc.reshape(width, local_latents)
    squares_dec = jnp.square(w_dec.astype(jnp.float32))
    norm_base = jnp.sqrt(jnp.sum(squares_dec[:, :half], axis=1) + norm_eps)
    norm_inst = jnp.sqrt(jnp.sum(squares_dec[:, half:], axis=1) + norm_eps)
    norm_sum = norm_base + norm_inst
    column_ids = jnp.arange(width, dtype=jnp.int32)
    bias_row = b_dec.reshape(width)
    pre = jnp.dot(xg, wenc_flat, preferred_element_type=jnp.float32) + b_enc[None, :]
    act = jnp.maximum(pre, 0.0)
    feats = act * act
    feats16 = feats.astype(jnp.bfloat16)
    partial_value = jnp.dot(feats16, w_dec, preferred_element_type=jnp.float32)
    recon = lax.psum(partial_value.astype(jnp.bfloat16), "latent").astype(jnp.float32)
    err = (recon + bias_row[None, :] - xg.astype(jnp.float32)) * maskg[:, None]
    err16 = err.astype(jnp.bfloat16)
    err_share = lax.dynamic_slice_in_dim(err, first_row, share_rows, 0)
    square_sum = jnp.sum(err_share * err_share)
    feat_sum = jnp.sum(feats * maskg[:, None], axis=0)
    local_loss = square_sum + sparsity_weight * jnp.sum(feat_sum * norm_sum)
    dfeat = 2.0 * lax.dot_general(
        err16, w_dec, (((1,), (1,)), ((), ())), preferred_element_type=jnp.float32
    )
    dfeat = dfeat + sparsity_weight * maskg[:, None] * norm_sum[None, :]
    dpre16 = (dfeat * 2.0 * act).astype(jnp.bfloat16)
    enc_term = lax.dot_general(
        xg, dpre16, (((0,), (0,)), ((), ())), preferred_element_type=jnp.float32
    )
    enc_term = enc_term.reshape(2, half, local_latents)
    dec_term = 2.0 * lax.dot_general(
        feats16, err16, (((0,), (0,)), ((), ())), preferred_element_type=jnp.float32
    )
    scale = jnp.where(
        column_ids[None, :] < half, (feat_sum / norm_base)[:, None], (feat_sum / norm_inst)[:, None]
    )
    dec_term = dec_term + sparsity_weight * scale * w_dec.astype(jnp.float32)
    enc_total = lax.psum_scatter(
        enc_term.astype(jnp.bfloat16), "dp", scatter_dimension=1, tiled=True
    ).astype(jnp.float32)
    dec_total = lax.psum_scatter(
        dec_term.astype(jnp.bfloat16), "dp", scatter_dimension=1, tiled=True
    ).astype(jnp.float32)
    total, count = lax.psum((local_loss, own_count), ("dp", "latent"))
    factor = loss_scale / count
    grad_enc = (enc_total * factor).astype(jnp.bfloat16)
    grad_dec = (dec_total * factor).astype(jnp.bfloat16)
    loss = total / (count * width)
    return (grad_enc, grad_dec, loss)


def solution(mesh):
    return jax.shard_map(
        shards,
        mesh=mesh,
        in_specs=(
            P(("dp", "latent"), None),
            P(("dp", "latent")),
            P(("dp", "latent"), None),
            P(None, None, "latent"),
            P("latent"),
            P("latent", None),
            P(),
        ),
        out_specs=(P(None, "dp", "latent"), P("latent", "dp"), P()),
        check_vma=False,
    )
```

profile of v0, /device:TPU:1, one launch (start us, length us, event | category | flops | bytes accessed | tf_op | source)
XLA Modules:
  0.0 414.3 jit_solution(3964806186658669848)
XLA Ops:
  7.2 0.0 copy-start
  7.2 0.0 all-gather.3.cloned.1.call-start
  7.2 1.6 sort.17
  8.9 0.0 copy-done
  8.9 0.6 gather_fusion
  9.5 0.5 broadcast.57
  10.0 0.7 reduce.2
  10.7 0.1 reshape.95
  10.8 10.1 %all_to_all.14 = bf16[4,2,4096]{2,1,0:T(2,128)(2,1)S(1)} all-to-all(bf16[4,2,4096]{2,1,0:T(2,128)(2,1)S(1)} %reshape.95), channel_id=1, replica_groups=mesh['dp'=4,'latent'=32] {'dp'}, dimensions={0} | all-to-all | bytes 131072 | tf_op jit(solution)/shard_map/all_to_all | solution.py:25
  20.9 0.7 reshape.96
  21.6 0.0 all-gather.3.cloned.1.call-update
  22.3 0.6 gather_fusion.1
  23.0 0.6 fusion.25
  23.6 0.7 copy.17
  24.3 3.2 all-to-all-start.1
  27.5 0.0 all-reduce.4.cloned.1.call-start
  27.5 1.3 dynamic-slice
  29.6 1.9 all-to-all-done.1
  31.5 0.1 reduce.1
  31.6 0.2 dynamic-update-slice
  31.8 65.9 %all-reduce = bf16[128]{0:T(256)(128)(2,1)S(1)} all-reduce(bf16[128]{0:T(256)(128)(2,1)S(1)} %dynamic-update-slice), channel_id=2, replica_groups=mesh['dp'=4,'latent'=32] {'latent'}, use_global_device_ids=true, to_apply=%add | all-reduce | flops 128 | bytes 512
  97.7 0.0 all-gather.3.cloned.1.call-done
  97.8 7.3 %multiply_reduce_fusion = (f32[512]{0:T(512)S(1)}, f32[128,512]{1,0:T(8,128)S(1)}) fusion(f32[128]{0:T(128)S(1)} %mul.102, f32[512]{0:T(512)} %param.11, bf16[8192,512]{1,0:T(8,128)(2,1)} %bitcast.33, bf16[128,1,8192]{2,1,0:T(2,128)(2,1)} %all-gather.3.cloned.1.call-done), kind=kOutput, calls=%fused_computation.26 | convolution fusion | flops 1074068992 | bytes 10752512 | tf_op jit(solution)/shard_map/dot_general | solution.py:44
  105.1 6.0 %convolution_convert_fusion = bf16[128,8192]{1,0:T(8,128)(2,1)} fusion(bf16[512,8192]{1,0:T(8,128)(2,1)} %param.12, f32[128,512]{1,0:T(8,128)S(1)} %get-tuple-element.16), kind=kOutput, calls=%fused_computation.6 | convolution fusion | flops 1074921472 | bytes 10747904 | tf_op jit(solution)/shard_map/dot_general | solution.py:48
  111.0 0.0 all-reduce.4.cloned.1.call-update
  111.1 0.0 copy-start.2
  111.1 0.2 reduce-scatter.3.cloned.1.call-start
  111.3 11.3 %convert_multiply_fusion.1 = f32[512,8192]{1,0:T(8,128)} fusion(bf16[512,8192]{1,0:T(8,128)(2,1)} %param.12), kind=kLoop, calls=%fused_computation.3 | loop fusion | flops 8388608 | bytes 25165824 | tf_op jit(solution)/shard_map/square | solution.py:38
  122.6 0.0 copy-done.2
  122.6 6.5 %slice_reduce_fusion.1 = (f32[512]{0:T(512)S(1)}, f32[512]{0:T(512)S(1)}) fusion(f32[512,8192]{1,0:T(8,128)} %convert_multiply_fusion.1), kind=kLoop, calls=%fused_computation.8 | loop fusion | flops 4193280 | bytes 16781312 | tf_op jit(solution)/shard_map/reduce_sum | solution.py:39
  129.2 8.8 %copy.19 = bf16[128,1,8192]{0,2,1:T(8,128)(2,1)S(1)} copy(bf16[128,1,8192]{2,1,0:T(2,128)(2,1)} %all-gather.3.cloned.1.call-done) | data formatting | bytes 4194304 | tf_op jit(solution)/shard_map/dot_general | solution.py:61
  138.0 0.6 multiply_reduce_fusion.2
  138.6 75.9 %all-reduce.4.cloned.1.call-done = bf16[128,8192]{1,0:T(8,128)(2,1)} async-done(((bf16[128,8192]{1,0:T(8,128)(2,1)}), bf16[128,8192]{1,0:T(8,128)(2,1)}) %all-reduce.4.cloned.1.call-update) | async-done | bytes 2097168 | tf_op jit(solution)/shard_map/psum | solution.py:49
  214.5 8.7 %subtract_multiply_fusion = f32[128,8192]{1,0:T(8,128)} fusion(bf16[128,8192]{1,0:T(8,128)(2,1)} %all-reduce.4.cloned.1.call-done, f32[128]{0:T(128)S(1)} %mul.102, f32[8192]{0:T(1024)S(1)} %bitcast.36, bf16[128,1,8192]{2,1,0:T(2,128)(2,1)} %all-gather.3.cloned.1.call-done), kind=kLoop, calls=%fused_computation.12 | loop fusion | flops 5242880 | bytes 8421888 | tf_op jit(solution)/shard_map/mul | solution.py:50
  223.2 15.0 %convolution_convert_fusion.1 = bf16[2,4096,512]{2,1,0:T(8,128)(2,1)} fusion(bf16[2,4096,128]{2,1,0:T(8,128)(2,1)S(1)} %bitcast.34, f32[128,512]{1,0:T(8,128)S(1)} %get-tuple-element.16, bf16[512,8192]{1,0:T(8,128)(2,1)} %param.12, f32[128,8192]{1,0:T(8,128)} %subtract_multiply_fusion, f32[512]{0:T(512)S(1)} %get-tuple-element.10, f32[128]{0:T(128)S(1)} %mul.102), kind=kOutput, calls=%fused_computation.9 | convolution fusion | flops 2153119744 | bytes 23333376 | tf_op jit(solution)/shard_map/dot_general | solution.py:61
  238.2 0.0 reduce-scatter.3.cloned.1.call-update
  238.2 0.0 reduce-scatter.5.cloned.1.call-start
  238.3 9.8 %fusion.1 = bf16[512,8192]{1,0:T(8,128)(2,1)} fusion(bf16[512,8192]{1,0:T(8,128)(2,1)} %param.12, f32[512]{0:T(512)S(1)} %get-tuple-element.12, f32[512]{0:T(512)S(1)} %get-tuple-element.11, pred[8192]{0:T(1024)(128)(4,1)S(1)} %iota_compare_fusion, f32[128,8192]{1,0:T(8,128)} %subtract_multiply_fusion, f32[128,512]{1,0:T(8,128)S(1)} %get-tuple-element.16), kind=kOutput, calls=%fused_computation.5 | convolution fusion | flops 1100087296 | bytes 21245952 | tf_op jit(solution)/shard_map/dot_general | solution.py:65
  248.0 0.0 reduce-scatter.5.cloned.1.call-update
  248.1 1.6 multiply_reduce_fusion.1
  251.0 69.5 %all-reduce.1 = (f32[]{:T(128)}, f32[]{:T(128)}) all-reduce(f32[]{:T(128)} %get-tuple-element.13, f32[]{:T(128)S(6)} %add.86), channel_id=1, replica_groups=mesh['dp'=4,'latent'=32] {'dp','latent'}, use_global_device_ids=true, to_apply=%region_6.7 | all-reduce | flops 2 | bytes 16 | tf_op jit(solution)/shard_map/psum | solution.py:78
  321.8 0.0 copy-start.1
  322.5 0.0 reduce-scatter.3.cloned.1.call-done
  322.5 3.3 multiply_convert_fusion.1
  325.8 77.3 %reduce-scatter.5.cloned.1.call-done = bf16[512,2048]{1,0:T(8,128)(2,1)} async-done(((bf16[512,8192]{1,0:T(8,128)(2,1)}), bf16[512,2048]{1,0:T(8,128)(2,1)}) %reduce-scatter.5.cloned.1.call-update) | async-done | bytes 2097168 | tf_op jit(solution)/shard_map/reduce_scatter | solution.py:75
  403.2 3.4 multiply_convert_fusion
  406.6 0.0 copy-done.1
  (8 shorter events, 0.0 us)
Async XLA Ops:
  7.2 1.7 copy-start
  7.2 90.6 %all-gather.3.cloned.1.call-start = ((), (), s32[]{:S(2)}) async-start(), calls=%async_computation.4 | async-start | bytes 4325376 | tf_op jit(solution)/shard_map/all_gather | solution.py:29
  24.3 7.2 %all-to-all-start.1 = ((bf16[4,1,1]{2,1,0:T(2,128)(2,1)}), bf16[4,1,1]{2,1,0:T(2,128)(2,1)S(1)}, u32[]{:S(2)}, u32[]{:S(2)}) async-start(bf16[4,1,1]{2,1,0:T(2,128)(2,1)} %copy.17), calls=%async_computation.1 | async-start | bytes 4096 | tf_op jit(solution)/shard_map/all_to_all | solution.py:26
  27.5 187.0 %all-reduce.4.cloned.1.call-start = ((), (), s32[]{:S(2)}) async-start(), calls=%async_computation.5 | async-start | bytes 4194304 | tf_op jit(solution)/shard_map/psum | solution.py:49
  111.1 11.6 %copy-start.2 = (f32[2,4096]{1,0:T(2,128)S(1)}, f32[2,4096]{1,0:T(2,128)}, u32[]{:S(2)}) copy-start(f32[2,4096]{1,0:T(2,128)} %param.13) | copy-start | bytes 98308
  111.1 211.4 %reduce-scatter.3.cloned.1.call-start = ((), (), s32[]{:S(2)}) async-start(), calls=%async_computation.6 | async-start | bytes 10485760 | tf_op jit(solution)/shard_map/reduce_scatter | solution.py:72
  238.2 165.0 %reduce-scatter.5.cloned.1.call-start = ((), (), s32[]{:S(2)}) async-start(), calls=%async_computation.7 | async-start | bytes 10485760 | tf_op jit(solution)/shard_map/reduce_scatter | solution.py:75
  321.8 84.8 %copy-start.1 = (bf16[5,8192]{1,0:T(8,128)(2,1)S(1)}, bf16[5,8192]{1,0:T(8,128)(2,1)}, u32[]{:S(2)}) copy-start(bf16[5,8192]{1,0:T(8,128)(2,1)} %param.7) | copy-start | bytes 245764
Sparse Core Ops, SparseCore 0:
  21.8 47.3 all-gather.2
  111.2 103.2 all-reduce.3
  238.3 82.5 reduce-scatter.2
  323.2 79.8 reduce-scatter.4
where the time goes:
time: 415 us; the launch traced here: 414 us
  waiting for transfers between devices  155 us (37%)
  blocking collectives  145 us (35%)
  other arithmetic  38.6 us (9%)
  matrix products  38 us (9%)
  between operations  19.7 us (5%)
  local copies, waits for them, and re-layouts  13.6 us (3%)
    reduce_scatter x1, waiting for transfers between devices, shards(): lax.psum_scatter(dec_term.astype(jnp.bfloat16), 'dp', scatter_dimension=1...  77.3 us
    psum x1, waiting for transfers between devices, shards(): lax.psum(partial_value.astype(jnp.bfloat16), 'latent').astype(jnp.float32)  75.9 us
    psum x1, blocking collectives, shards(): total, count = lax.psum((local_loss, own_count), ('dp', 'latent'))  69.5 us
    unnamed x1, blocking collectives  65.9 us
    dot_general x1, matrix products, shards(): lax.dot_general(xg, dpre16, (((0,), (0,)), ((), ())), preferred_element_t...  15 us
    square x1, other arithmetic, shards(): squares_dec = jnp.square(w_dec.astype(jnp.float32))  11.3 us
    all_to_all x1, blocking collectives, shards(): lax.all_to_all(outgoing, 'dp', split_axis=0, concat_axis=0, tiled=True)  10.1 us
    dot_general x1, matrix products, shards(): lax.dot_general(feats16, err16, (((0,), (0,)), ((), ())), preferred_eleme...  9.77 us
  transfers between devices with their start and end apart: 5, of which 3 were waited for; matrix products, arithmetic and copies ran while one was open for 11% of the time, Pallas kernels for 0%

commit v1 on v0

--- a/solution.py
+++ b/solution.py
@@ -9,6 +9,11 @@
 
 
 def shards(acts, chat_len, group_of, w_enc, b_enc, w_dec, b_dec):
+
+    def _draw_yards(s0, peer_axis):
+        a_next = lax.all_gather(s0, peer_axis)
+        return jnp.sum(a_next, axis=0)
+
     groups = lax.axis_size("dp")
     slots = acts.shape[0]
     width = acts.shape[1]
@@ -46,7 +51,7 @@
     feats = act * act
     feats16 = feats.astype(jnp.bfloat16)
     partial_value = jnp.dot(feats16, w_dec, preferred_element_type=jnp.float32)
-    recon = lax.psum(partial_value.astype(jnp.bfloat16), "latent").astype(jnp.float32)
+    recon = _draw_yards(partial_value.astype(jnp.bfloat16), "latent").astype(jnp.float32)
     err = (recon + bias_row[None, :] - xg.astype(jnp.float32)) * maskg[:, None]
     err16 = err.astype(jnp.bfloat16)
     err_share = lax.dynamic_slice_in_dim(err, first_row, share_rows, 0)

time: 415 us -> 521 us (1.26)
  waiting for transfers between devices: 155 us -> 242 us
  other arithmetic: 38.6 us -> 58.7 us
    all_gather x0 -> x1, waiting for transfers between devices: none -> 177 us  [_draw_yards(): a_next = lax.all_gather(s0, peer_axis)]
    reduce_scatter x1, waiting for transfers between devices: 77.3 us -> 0.02 us  [shards(): lax.psum_scatter(dec_term.astype(jnp.bfloat16), 'dp', scatter_dimension=1...]
    psum x1 -> x0, waiting for transfers between devices: 75.9 us -> none  [shards(): lax.psum(partial_value.astype(jnp.bfloat16), 'latent').astype(jnp.float32)]
    reduce_scatter x1, waiting for transfers between devices: 0.02 us -> 62.6 us  [shards(): lax.psum_scatter(enc_term.astype(jnp.bfloat16), 'dp', scatter_dimension=1...]
    reduce_sum x0 -> x1, other arithmetic: none -> 21.2 us  [_draw_yards(): return jnp.sum(a_next, axis=0)]
  transfers between devices with their start and end apart: 5 -> 5, of which waited for: 3 -> 3; matrix products, arithmetic and copies ran while one was open for 11% -> 10% of each run, Pallas kernels for 0% -> 0%
where the time goes in v1:
time: 521 us
  waiting for transfers between devices  242 us (46%)
  blocking collectives  144 us (28%)
  other arithmetic  58.7 us (11%)
  matrix products  36.7 us (7%)
  between operations  19.7 us (4%)
  local copies, waits for them, and re-layouts  15.6 us (3%)
    all_gather x1, waiting for transfers between devices, _draw_yards(): a_next = lax.all_gather(s0, peer_axis)  177 us
    psum x1, blocking collectives, shards(): total, count = lax.psum((local_loss, own_count), ('dp', 'latent'))  68.1 us
    unnamed x1, blocking collectives  65.9 us
    reduce_scatter x1, waiting for transfers between devices, shards(): lax.psum_scatter(enc_term.astype(jnp.bfloat16), 'dp', scatter_dimension=1...  62.6 us
    reduce_sum x1, other arithmetic, _draw_yards(): return jnp.sum(a_next, axis=0)  21.2 us
    dot_general x1, matrix products, shards(): lax.dot_general(xg, dpre16, (((0,), (0,)), ((), ())), preferred_element_t...  15 us
    square x1, other arithmetic, shards(): squares_dec = jnp.square(w_dec.astype(jnp.float32))  12.9 us
  transfers between devices with their start and end apart: 5, of which 3 were waited for; matrix products, arithmetic and copies ran while one was open for 10% of the time, Pallas kernels for 0%

profile of v1, /device:TPU:1, one launch (start us, length us, event | category | flops | bytes accessed | tf_op | source)
XLA Modules:
  0.0 520.7 jit_solution(2419714381190917674)
XLA Ops:
  7.2 0.0 copy-start
  7.2 0.0 all-gather.5.cloned.1.call-start
  7.2 1.6 sort.17
  8.9 0.0 copy-done
  8.9 0.6 gather_fusion
  9.5 0.5 broadcast.57
  10.0 0.7 reduce.3
  10.7 0.1 reshape.96
  10.8 10.1 %all_to_all.14 = bf16[4,2,4096]{2,1,0:T(2,128)(2,1)S(1)} all-to-all(bf16[4,2,4096]{2,1,0:T(2,128)(2,1)S(1)} %reshape.96), channel_id=1, replica_groups=mesh['dp'=4,'latent'=32] {'dp'}, dimensions={0} | all-to-all | bytes 131072 | tf_op jit(solution)/shard_map/all_to_all | solution.py:30
  20.9 0.7 reshape.97
  21.6 0.0 all-gather.5.cloned.1.call-update
  22.3 0.6 gather_fusion.1
  23.0 0.6 fusion.25
  23.6 0.7 copy.17
  24.3 3.2 all-to-all-start.1
  27.5 0.0 all-gather.7.cloned.1.call-start
  27.5 1.3 dynamic-slice
  29.6 1.9 all-to-all-done.1
  31.5 0.1 reduce.2
  31.6 0.2 dynamic-update-slice
  31.8 65.9 %all-reduce = bf16[128]{0:T(256)(128)(2,1)S(1)} all-reduce(bf16[128]{0:T(256)(128)(2,1)S(1)} %dynamic-update-slice), channel_id=3, replica_groups=mesh['dp'=4,'latent'=32] {'latent'}, use_global_device_ids=true, to_apply=%add | all-reduce | flops 128 | bytes 512
  97.7 0.0 all-gather.5.cloned.1.call-done
  97.8 7.3 %multiply_reduce_fusion = (f32[512]{0:T(512)S(1)}, f32[128,512]{1,0:T(8,128)S(1)}) fusion(f32[128]{0:T(128)S(1)} %mul.102, f32[512]{0:T(512)} %param.11, bf16[8192,512]{1,0:T(8,128)(2,1)} %bitcast.34, bf16[128,1,8192]{2,1,0:T(2,128)(2,1)} %all-gather.5.cloned.1.call-done), kind=kOutput, calls=%fused_computation.26 | convolution fusion | flops 1074068992 | bytes 10752512 | tf_op jit(solution)/shard_map/dot_general | solution.py:49
  105.1 0.0 copy-start.3
  105.1 6.0 %convolution_convert_fusion = bf16[128,8192]{1,0:T(8,128)(2,1)} fusion(bf16[512,8192]{1,0:T(8,128)(2,1)} %param.12, f32[128,512]{1,0:T(8,128)S(1)} %get-tuple-element.16), kind=kOutput, calls=%fused_computation.6 | convolution fusion | flops 1074921472 | bytes 10747904 | tf_op jit(solution)/shard_map/dot_general | solution.py:53
  111.0 0.0 all-gather.7.cloned.1.call-update
  111.1 0.2 reduce-scatter.5.cloned.1.call-start
  111.3 12.9 %convert_multiply_fusion.1 = f32[512,8192]{1,0:T(8,128)} fusion(bf16[512,8192]{1,0:T(8,128)(2,1)} %param.12), kind=kLoop, calls=%fused_computation.3 | loop fusion | flops 8388608 | bytes 25165824 | tf_op jit(solution)/shard_map/square | solution.py:43
  124.2 6.5 %slice_reduce_fusion.1 = (f32[512]{0:T(512)S(1)}, f32[512]{0:T(512)S(1)}) fusion(f32[512,8192]{1,0:T(8,128)} %convert_multiply_fusion.1), kind=kLoop, calls=%fused_computation.8 | loop fusion | flops 4193280 | bytes 16781312 | tf_op jit(solution)/shard_map/reduce_sum | solution.py:44
  130.7 0.6 multiply_reduce_fusion.2
  131.3 177.4 %all-gather.7.cloned.1.call-done = bf16[4096,8192]{1,0:T(8,128)(2,1)} async-done(((bf16[128,8192]{1,0:T(8,128)(2,1)}), bf16[4096,8192]{1,0:T(8,128)(2,1)}) %all-gather.7.cloned.1.call-update) | async-done | bytes 67108880 | tf_op jit(solution)/shard_map/all_gather | solution.py:14
  308.7 21.2 %reduce_sum.66 = bf16[128,8192]{1,0:T(8,128)(2,1)S(1)} reduce(bf16[32,128,8192]{2,1,0:T(8,128)(2,1)} %bitcast.5, bf16[]{:T(256)} %constant.2.clone.1), dimensions={0}, to_apply=%region_1.2 | reduce | flops 32505856 | bytes 69206016 | tf_op jit(solution)/shard_map/reduce_sum | solution.py:15
  329.9 6.1 %subtract_multiply_fusion = f32[128,8192]{1,0:T(8,128)S(1)} fusion(bf16[128,8192]{1,0:T(8,128)(2,1)S(1)} %reduce_sum.66, f32[128]{0:T(128)S(1)} %mul.102, f32[8192]{0:T(1024)S(1)} %bitcast.37, bf16[128,1,8192]{2,1,0:T(2,128)(2,1)} %all-gather.5.cloned.1.call-done), kind=kLoop, calls=%fused_computation.12 | loop fusion | flops 5242880 | bytes 8421888 | tf_op jit(solution)/shard_map/mul | solution.py:55
  336.0 0.0 copy-start.2
  336.0 1.9 copy-done.2
  338.0 8.4 %fusion.1 = bf16[512,8192]{1,0:T(8,128)(2,1)} fusion(bf16[512,8192]{1,0:T(8,128)(2,1)} %param.12, f32[512]{0:T(512)S(1)} %get-tuple-element.12, f32[512]{0:T(512)S(1)} %get-tuple-element.11, pred[8192]{0:T(1024)(128)(4,1)S(1)} %iota_compare_fusion, f32[128,8192]{1,0:T(8,128)S(1)} %subtract_multiply_fusion, f32[128,512]{1,0:T(8,128)S(1)} %get-tuple-element.16), kind=kOutput, calls=%fused_computation.5 | convolution fusion | flops 1100087296 | bytes 21245952 | tf_op jit(solution)/shard_map/dot_general | solution.py:70
  346.4 0.0 reduce-scatter.5.cloned.1.call-update
  346.4 0.3 reduce-scatter.3.cloned.1.call-start
  346.7 8.9 %copy.19 = bf16[128,1,8192]{0,2,1:T(8,128)(2,1)S(1)} copy(bf16[128,1,8192]{2,1,0:T(2,128)(2,1)} %all-gather.5.cloned.1.call-done) | data formatting | bytes 4194304 | tf_op jit(solution)/shard_map/dot_general | solution.py:66
  355.6 15.0 %convolution_convert_fusion.1 = bf16[2,4096,512]{2,1,0:T(8,128)(2,1)} fusion(bf16[2,4096,128]{2,1,0:T(8,128)(2,1)S(1)} %bitcast.35, f32[128,512]{1,0:T(8,128)S(1)} %get-tuple-element.16, bf16[512,8192]{1,0:T(8,128)(2,1)} %param.12, f32[128,8192]{1,0:T(8,128)} %copy-done.2, f32[512]{0:T(512)S(1)} %get-tuple-element.10, f32[128]{0:T(128)S(1)} %mul.102), kind=kOutput, calls=%fused_computation.9 | convolution fusion | flops 2153119744 | bytes 23333376 | tf_op jit(solution)/shard_map/dot_general | solution.py:66
  370.5 0.0 reduce-scatter.3.cloned.1.call-update
  370.5 1.6 multiply_reduce_fusion.1
  373.5 68.1 %all-reduce.1 = (f32[]{:T(128)}, f32[]{:T(128)}) all-reduce(f32[]{:T(128)} %get-tuple-element.13, f32[]{:T(128)S(6)} %add.84), channel_id=1, replica_groups=mesh['dp'=4,'latent'=32] {'dp','latent'}, use_global_device_ids=true, to_apply=%region_6.7 | all-reduce | flops 2 | bytes 16 | tf_op jit(solution)/shard_map/psum | solution.py:83
  442.9 0.0 copy-start.1
  443.6 0.0 reduce-scatter.5.cloned.1.call-done
  443.6 3.4 multiply_convert_fusion
  447.1 62.6 %reduce-scatter.3.cloned.1.call-done = bf16[2,1024,512]{2,1,0:T(8,128)(2,1)} async-done(((bf16[2,4096,512]{2,1,0:T(8,128)(2,1)}), bf16[2,1024,512]{2,1,0:T(8,128)(2,1)}) %reduce-scatter.3.cloned.1.call-update) | async-done | bytes 2097168 | tf_op jit(solution)/shard_map/reduce_scatter | solution.py:77
  509.7 3.3 multiply_convert_fusion.1
  (10 shorter events, 0.0 us)
Async XLA Ops:
  7.2 1.7 copy-start
  7.2 90.6 %all-gather.5.cloned.1.call-start = ((), (), s32[]{:S(2)}) async-start(), calls=%async_computation.4 | async-start | bytes 4325376 | tf_op jit(solution)/shard_map/all_gather | solution.py:34
  24.3 7.2 %all-to-all-start.1 = ((bf16[4,1,1]{2,1,0:T(2,128)(2,1)}), bf16[4,1,1]{2,1,0:T(2,128)(2,1)S(1)}, u32[]{:S(2)}, u32[]{:S(2)}) async-start(bf16[4,1,1]{2,1,0:T(2,128)(2,1)} %copy.17), calls=%async_computation.1 | async-start | bytes 4096 | tf_op jit(solution)/shard_map/all_to_all | solution.py:31
  27.5 281.2 %all-gather.7.cloned.1.call-start = ((), (), s32[]{:S(2)}) async-start(), calls=%async_computation.7 | async-start | bytes 69206016 | tf_op jit(solution)/shard_map/all_gather | solution.py:14
  105.1 6.2 %copy-start.3 = (f32[2,4096]{1,0:T(2,128)S(1)}, f32[2,4096]{1,0:T(2,128)}, u32[]{:S(2)}) copy-start(f32[2,4096]{1,0:T(2,128)} %param.13) | copy-start | bytes 98308
  111.1 332.6 %reduce-scatter.5.cloned.1.call-start = ((), (), s32[]{:S(2)}) async-start(), calls=%async_computation.6 | async-start | bytes 10485760 | tf_op jit(solution)/shard_map/reduce_scatter | solution.py:80
  336.0 1.9 copy-start.2
  346.4 163.3 %reduce-scatter.3.cloned.1.call-start = ((), (), s32[]{:S(2)}) async-start(), calls=%async_computation.5 | async-start | bytes 10485760 | tf_op jit(solution)/shard_map/reduce_scatter | solution.py:77
  442.9 70.1 %copy-start.1 = (bf16[5,8192]{1,0:T(8,128)(2,1)S(1)}, bf16[5,8192]{1,0:T(8,128)(2,1)}, u32[]{:S(2)}) copy-start(bf16[5,8192]{1,0:T(8,128)(2,1)} %param.7) | copy-start | bytes 245764
Sparse Core Ops, SparseCore 0:
  21.8 47.3 all-gather.4
  111.2 197.4 all-gather.6
  346.5 80.7 reduce-scatter.4
  429.6 80.0 reduce-scatter.2
